TPU v7x, 32 devices: a whole 2x2x4 slice. The times are simulated.
32 devices in a mesh: dp: 8 (over z, x), mp: 4 (over y, core).
Axes of the slice: x: 2, y: 2, z: 4, core: 2. Of those that a mesh axis runs over, the one named last changes fastest.
Arguments:
- mel_frames: float32 [16384, 80], P('dp')
- frame_mask: int32 [8, 1024], replicated, may hold values from 0 to 1, as said below
- token_ids: int32 [8, 384], replicated, may hold values from 0 to 51839
- token_mask: int32 [8, 384], replicated, may hold values from 0 to 1, as said below
- embedding: float32 [51840, 768], P('dp', 'mp'), may hold values from -6 to 6
- conv_one: float32 [3, 80, 768], P(None, None, ('dp', 'mp')), may hold values from -0.375 to 0.375
- conv_two: float32 [3, 768, 768], P(None, ('dp', 'mp')), may hold values from -0.125 to 0.125
- enc_qkv: float32 [3, 768, 768], P(None, 'dp', 'mp'), may hold values from -0.21875 to 0.21875
- enc_out: float32 [768, 768], P('mp', 'dp'), may hold values from -3.5 to 3.5
- enc_up: float32 [768, 3072], P('dp', 'mp'), may hold values from -0.21875 to 0.21875
- enc_down: float32 [3072, 768], P('mp', 'dp'), may hold values from -0.109375 to 0.109375
- cross_qkv: float32 [3, 768, 768], P(None, 'dp', 'mp'), may hold values from -0.21875 to 0.21875
- cross_out: float32 [768, 768], P('mp', 'dp'), may hold values from -3.5 to 3.5
- dec_qkv: float32 [3, 768, 768], P(None, 'dp', 'mp'), may hold values from -0.21875 to 0.21875
- dec_out: float32 [768, 768], P('mp', 'dp'), may hold values from -1.75 to 1.75
- dec_up: float32 [768, 3072], P('dp', 'mp'), may hold values from -0.21875 to 0.21875
- dec_down: float32 [3072, 768], P('mp', 'dp'), may hold values from -0.109375 to 0.109375
- norm_params: float32 [6, 2, 768], P(None, None, 'dp'), as said below
- cotangent: float32 [3072, 768], P('dp'), may hold values from -6 to 6
Outputs:
- decoded: float32 [3072, 768], P('dp')
- mel_grad: float32 [16384, 80], P('dp')
- embed_grad: float32 [51840, 768], P('dp', 'mp')
- conv_one_grad: float32 [3, 80, 768], P(None, None, ('dp', 'mp'))
- conv_two_grad: float32 [3, 768, 768], P(None, ('dp', 'mp'))
- enc_qkv_grad: float32 [3, 768, 768], P(None, 'dp', 'mp')
- enc_out_grad: float32 [768, 768], P('mp', 'dp')
- enc_up_grad: float32 [768, 3072], P('dp', 'mp')
- enc_down_grad: float32 [3072, 768], P('mp', 'dp')
- cross_qkv_grad: float32 [3, 768, 768], P(None, 'dp', 'mp')
- cross_out_grad: float32 [768, 768], P('mp', 'dp')
- dec_qkv_grad: float32 [3, 768, 768], P(None, 'dp', 'mp')
- dec_out_grad: float32 [768, 768], P('mp', 'dp')
- dec_up_grad: float32 [768, 3072], P('dp', 'mp')
- dec_down_grad: float32 [3072, 768], P('mp', 'dp')
- norm_grad: float32 [6, 2, 768], P(None, None, 'dp')
- rms_stats: float32 [9], replicated
Inputs may be any that keep to these rules, and one draw needn't show every extreme that they name: `frame_mask`: each clip's row is 1 on a prefix of at least max(68, 1) frames and 0 after it; some clip is valid in full. `token_mask`: each clip's row is 1 on a prefix of at least max(24, 1) tokens and 0 after it; some clip is valid in full. `norm_params`: gains near one and biases near zero.
All inputs are finite; a program needn't handle non-finite values.
Results may differ from a plain program's by a relative error of at most 0.0003.
Values sent between devices are 32-bit elements; how exact they have to be, the bound alone decides.
A program may use at most 256 MiB of HBM per device.

v0:
```python
import math
import jax
import jax.numpy as jnp
from jax import lax
from jax.sharding import PartitionSpec as P

HEAD = 64
HIGH = lax.Precision.HIGHEST
NEG = -1e30
EPS = 1e-05


def matmul(left, right):
    return jnp.dot(left, right, precision=HIGH, preferred_element_type=jnp.float32)


def gelu_exact(tensor):
    return jax.nn.gelu(tensor, approximate=False)


def layer_norm(tensor, norm_param):
    centre = tensor - jnp.mean(tensor, axis=-1, keepdims=True)
    spread = jnp.mean(centre * centre, axis=-1, keepdims=True)
    return centre * lax.rsqrt(spread + EPS) * norm_param[0] + norm_param[1]


def sinusoid(position, model_width):
    half_width = model_width // 2
    inverse_rates = jnp.exp(
        -math.log(10000.0) * jnp.arange(half_width).astype(jnp.float32) / (half_width - 1)
    )
    angles = position.astype(jnp.float32)[:, None] * inverse_rates[None, :]
    return jnp.concatenate([jnp.sin(angles), jnp.cos(angles)], axis=1)


def split_heads(tensor):
    return tensor.reshape(tensor.shape[0], -1, HEAD)


def attend(queries, key_rows, values, allowed):
    factor = 1.0 / math.sqrt(queries.shape[-1])
    scores = jnp.einsum("qhe,khe->hqk", queries, key_rows, precision=HIGH) * factor
    scores = jnp.where(allowed[None], scores, NEG)
    peaks = jnp.max(scores, axis=-1, keepdims=True)
    weight = jnp.exp(scores - peaks)
    totals = jnp.sum(weight, axis=-1, keepdims=True)
    output = jnp.einsum("hqk,khe->qhe", weight / totals, values, precision=HIGH)
    return (output, peaks + jnp.log(totals))


def attention_grads(queries, key_rows, values, allowed, output, log_total, grad_flat):
    factor = 1.0 / math.sqrt(queries.shape[-1])
    grad_out = grad_flat.reshape(output.shape)
    scores = jnp.einsum("qhe,khe->hqk", queries, key_rows, precision=HIGH) * factor
    attn_probs = jnp.where(allowed[None], jnp.exp(scores - log_total), 0.0)
    grad_values = jnp.einsum("hqk,qhe->khe", attn_probs, grad_out, precision=HIGH)
    grad_probs = jnp.einsum("qhe,khe->hqk", grad_out, values, precision=HIGH)
    inner_dot = jnp.sum(grad_out * output, axis=-1)
    grad_scores = attn_probs * (grad_probs - inner_dot.T[:, :, None]) * factor
    grad_queries = jnp.einsum("hqk,khe->qhe", grad_scores, key_rows, precision=HIGH)
    grad_keys = jnp.einsum("hqk,qhe->khe", grad_scores, queries, precision=HIGH)
    return (
        grad_queries.reshape(grad_queries.shape[0], -1),
        grad_keys.reshape(grad_keys.shape[0], -1),
        grad_values.reshape(grad_values.shape[0], -1),
    )


def project_three(rows_in, norm_param, weight):
    normed = layer_norm(rows_in, norm_param)
    return (matmul(normed, weight[0]), matmul(normed, weight[1]), matmul(normed, weight[2]))


def project_pair(rows_in, norm_param, weight_keys, weight_values):
    normed = layer_norm(rows_in, norm_param)
    return (matmul(normed, weight_keys), matmul(normed, weight_values))


def project_one(rows_in, norm_param, weight):
    return matmul(layer_norm(rows_in, norm_param), weight)


def feed_forward(rows_in, norm_param, up_weight, down_weight):
    return matmul(gelu_exact(matmul(layer_norm(rows_in, norm_param), up_weight)), down_weight)


def stem_piece(mel_in, weight_one, weight_two):
    mel_rows = mel_in.shape[0]
    padded = jnp.pad(mel_in, ((1, 1), (0, 0)))
    activated = gelu_exact(
        matmul(padded[0:mel_rows], weight_one[0])
        + matmul(padded[1 : mel_rows + 1], weight_one[1])
        + matmul(padded[2 : mel_rows + 2], weight_one[2])
    )
    padded_one = jnp.pad(activated, ((1, 1), (0, 0)))
    return (
        matmul(padded_one[0:mel_rows:2], weight_two[0])
        + matmul(padded_one[1 : mel_rows + 1 : 2], weight_two[1])
        + matmul(padded_one[2 : mel_rows + 2 : 2], weight_two[2])
    )


def masked_squares(tensor, row_weight):
    return jnp.sum(row_weight[:, None] * tensor * tensor)


def branch_sum(tensor):
    return lax.psum(tensor, "mp")


def input_sum(grad_rows, grad_norm):
    return lax.psum((grad_rows, grad_norm), "mp")


def body(
    mel_frames,
    frame_mask,
    token_ids,
    token_mask,
    embedding,
    conv_one,
    conv_two,
    enc_qkv,
    enc_out,
    enc_up,
    enc_down,
    cross_qkv,
    cross_out,
    dec_qkv,
    dec_out,
    dec_up,
    dec_down,
    norm_params,
    cotangent,
):
    dp_place = lax.axis_index("dp")
    frames = mel_frames.shape[0] // 2
    tokens = cotangent.shape[0]
    model_width = cotangent.shape[1]
    gathered = (
        lax.all_gather(conv_one, "dp", axis=2, tiled=True),
        lax.all_gather(conv_two, "dp", axis=1, tiled=True),
        lax.all_gather(enc_qkv, "dp", axis=1, tiled=True),
        lax.all_gather(enc_out, "dp", axis=1, tiled=True),
        lax.all_gather(enc_up, "dp", axis=0, tiled=True),
        lax.all_gather(enc_down, "dp", axis=1, tiled=True),
        lax.all_gather(cross_qkv, "dp", axis=1, tiled=True),
        lax.all_gather(cross_out, "dp", axis=1, tiled=True),
        lax.all_gather(dec_qkv, "dp", axis=1, tiled=True),
        lax.all_gather(dec_out, "dp", axis=1, tiled=True),
        lax.all_gather(dec_up, "dp", axis=0, tiled=True),
        lax.all_gather(dec_down, "dp", axis=1, tiled=True),
        lax.all_gather(norm_params, "dp", axis=2, tiled=True),
    )
    (
        full_conv_one,
        full_conv_two,
        full_enc_qkv,
        full_enc_out,
        full_enc_up,
        full_enc_down,
        full_cross_qkv,
        full_cross_out,
        full_dec_qkv,
        full_dec_out,
        full_dec_up,
        full_dec_down,
        full_norms,
    ) = gathered
    frame_row = lax.dynamic_index_in_dim(frame_mask, dp_place, 0, keepdims=False) > 0
    token_row = lax.dynamic_index_in_dim(token_mask, dp_place, 0, keepdims=False) > 0
    frame_allowed = frame_row[None, :]
    stem_sum = branch_sum(stem_piece(mel_frames, full_conv_one, full_conv_two))
    stream_zero = gelu_exact(stem_sum) + sinusoid(jnp.arange(frames, dtype=jnp.int32), model_width)
    enc_query, enc_keys, enc_values = project_three(stream_zero, full_norms[0], full_enc_qkv)
    enc_query_heads = split_heads(enc_query)
    enc_key_all = split_heads(enc_keys)
    enc_value_all = split_heads(enc_values)
    enc_mixed, enc_log_total = attend(enc_query_heads, enc_key_all, enc_value_all, frame_allowed)
    enc_mixed_flat = enc_mixed.reshape(frames, -1)
    enc_attn = branch_sum(matmul(enc_mixed_flat, full_enc_out))
    stream_one = stream_zero + enc_attn
    enc_mlp = branch_sum(feed_forward(stream_one, full_norms[1], full_enc_up, full_enc_down))
    stream_two = stream_one + enc_mlp
    cross_keys, cross_values = project_pair(
        stream_two, full_norms[2], full_cross_qkv[1], full_cross_qkv[2]
    )
    cross_key_all = split_heads(cross_keys)
    cross_value_all = split_heads(cross_values)
    flat_ids = token_ids.reshape(-1)
    vocab_rows = embedding.shape[0]
    local_ids = flat_ids - dp_place * vocab_rows
    owned_flags = (local_ids >= 0) & (local_ids < vocab_rows)
    safe_ids = jnp.clip(local_ids, 0, vocab_rows - 1)
    id_block = safe_ids
    flag_block = owned_flags
    picked = jnp.take(embedding, id_block, axis=0)
    embed_share = lax.psum_scatter(
        jnp.where(flag_block[:, None], picked, 0.0), "dp", scatter_dimension=0, tiled=True
    )
    embedded = lax.all_gather(embed_share, "mp", axis=1, tiled=True)
    text_zero = embedded + sinusoid(jnp.arange(tokens, dtype=jnp.int32), model_width)
    dec_query, dec_keys, dec_values = project_three(text_zero, full_norms[3], full_dec_qkv)
    positions = jnp.arange(tokens)
    self_allowed = (positions[None, :] <= positions[:, None]) & token_row[None, :]
    dec_query_heads = split_heads(dec_query)
    dec_key_all = split_heads(dec_keys)
    dec_value_all = split_heads(dec_values)
    dec_mixed, dec_log_total = attend(dec_query_heads, dec_key_all, dec_value_all, self_allowed)
    dec_mixed_flat = dec_mixed.reshape(tokens, -1)
    dec_attn = branch_sum(matmul(dec_mixed_flat, full_dec_out))
    text_one = text_zero + dec_attn
    cross_query = project_one(text_one, full_norms[4], full_cross_qkv[0])
    cross_query_heads = split_heads(cross_query)
    cross_mixed, cross_log_total = attend(
        cross_query_heads, cross_key_all, cross_value_all, frame_allowed
    )
    cross_mixed_flat = cross_mixed.reshape(tokens, -1)
    cross_attn = branch_sum(matmul(cross_mixed_flat, full_cross_out))
    text_two = text_one + cross_attn
    dec_mlp = branch_sum(feed_forward(text_two, full_norms[5], full_dec_up, full_dec_down))
    decoded = text_two + dec_mlp
    frame_weight = frame_row.astype(jnp.float32)
    token_weight = token_row.astype(jnp.float32)
    local_sums = jnp.stack(
        [
            masked_squares(stream_zero, frame_weight),
            masked_squares(enc_attn, frame_weight),
            masked_squares(enc_mlp, frame_weight),
            masked_squares(stream_two, frame_weight),
            masked_squares(text_zero, token_weight),
            masked_squares(dec_attn, token_weight),
            masked_squares(cross_attn, token_weight),
            masked_squares(dec_mlp, token_weight),
            masked_squares(decoded, token_weight),
        ]
    )
    square_sums = lax.psum(local_sums, "dp")
    frame_total = jnp.sum((frame_mask > 0).astype(jnp.float32))
    token_total = jnp.sum((token_mask > 0).astype(jnp.float32))
    counts = jnp.concatenate([jnp.full((4,), frame_total), jnp.full((5,), token_total)])
    rms_stats = jnp.sqrt(square_sums / (counts * model_width))
    grad_part, grad_norm_five, grad_dec_up, grad_dec_down = jax.vjp(
        feed_forward, text_two, full_norms[5], full_dec_up, full_dec_down
    )[1](cotangent)
    grad_summed, grad_norm_five = input_sum(grad_part, grad_norm_five)
    grad_text_two = cotangent + grad_summed
    grad_cross_out = matmul(cross_mixed_flat.T, grad_text_two)
    grad_cross_mixed = matmul(grad_text_two, full_cross_out.T)
    grad_cross_query, grad_cross_keys, grad_cross_values = attention_grads(
        cross_query_heads,
        cross_key_all,
        cross_value_all,
        frame_allowed,
        cross_mixed,
        cross_log_total,
        grad_cross_mixed,
    )
    grad_part, grad_norm_four, grad_cross_wq = jax.vjp(
        project_one, text_one, full_norms[4], full_cross_qkv[0]
    )[1](grad_cross_query)
    grad_summed, grad_norm_four = input_sum(grad_part, grad_norm_four)
    grad_text_one = grad_text_two + grad_summed
    grad_dec_out = matmul(dec_mixed_flat.T, grad_text_one)
    grad_dec_mixed = matmul(grad_text_one, full_dec_out.T)
    grad_dec_query, grad_dec_keys, grad_dec_values = attention_grads(
        dec_query_heads,
        dec_key_all,
        dec_value_all,
        self_allowed,
        dec_mixed,
        dec_log_total,
        grad_dec_mixed,
    )
    grad_part, grad_norm_three, grad_dec_qkv = jax.vjp(
        project_three, text_zero, full_norms[3], full_dec_qkv
    )[1]((grad_dec_query, grad_dec_keys, grad_dec_values))
    grad_summed, grad_norm_three = input_sum(grad_part, grad_norm_three)
    grad_text_zero = grad_text_one + grad_summed
    mp_place = lax.axis_index("mp")
    embed_width = embedding.shape[1]
    grad_embed_share = lax.dynamic_slice_in_dim(
        grad_text_zero, mp_place * embed_width, embed_width, 1
    )
    id_block = safe_ids
    flag_block = owned_flags
    grad_embedding = (
        jnp.zeros(embedding.shape, jnp.float32)
        .at[id_block]
        .add(
            jnp.where(
                flag_block[:, None], lax.all_gather(grad_embed_share, "dp", axis=0, tiled=True), 0.0
            )
        )
    )
    grad_part, grad_norm_two, grad_cross_wk, grad_cross_wv = jax.vjp(
        project_pair, stream_two, full_norms[2], full_cross_qkv[1], full_cross_qkv[2]
    )[1]((grad_cross_keys, grad_cross_values))
    grad_cross_qkv = jnp.stack([grad_cross_wq, grad_cross_wk, grad_cross_wv])
    grad_stream_two, grad_norm_two = input_sum(grad_part, grad_norm_two)
    grad_part, grad_norm_one, grad_enc_up, grad_enc_down = jax.vjp(
        feed_forward, stream_one, full_norms[1], full_enc_up, full_enc_down
    )[1](grad_stream_two)
    grad_summed, grad_norm_one = input_sum(grad_part, grad_norm_one)
    grad_stream_one = grad_stream_two + grad_summed
    grad_enc_out = matmul(enc_mixed_flat.T, grad_stream_one)
    grad_enc_mixed = matmul(grad_stream_one, full_enc_out.T)
    grad_enc_query, grad_enc_keys, grad_enc_values = attention_grads(
        enc_query_heads,
        enc_key_all,
        enc_value_all,
        frame_allowed,
        enc_mixed,
        enc_log_total,
        grad_enc_mixed,
    )
    grad_part, grad_norm_zero, grad_enc_qkv = jax.vjp(
        project_three, stream_zero, full_norms[0], full_enc_qkv
    )[1]((grad_enc_query, grad_enc_keys, grad_enc_values))
    grad_summed, grad_norm_zero = input_sum(grad_part, grad_norm_zero)
    grad_stream_zero = grad_stream_one + grad_summed
    grad_stem = jax.vjp(gelu_exact, stem_sum)[1](grad_stream_zero)[0]
    grad_mel_part, grad_conv_one, grad_conv_two = jax.vjp(
        stem_piece, mel_frames, full_conv_one, full_conv_two
    )[1](grad_stem)
    grad_mel = branch_sum(grad_mel_part)
    grad_norms = jnp.stack(
        [
            grad_norm_zero,
            grad_norm_one,
            grad_norm_two,
            grad_norm_three,
            grad_norm_four,
            grad_norm_five,
        ]
    )
    all_parts = tuple(
        (
            lax.psum_scatter(grad_conv_one, "dp", scatter_dimension=2, tiled=True),
            lax.psum_scatter(grad_conv_two, "dp", scatter_dimension=1, tiled=True),
            lax.psum_scatter(grad_enc_qkv, "dp", scatter_dimension=1, tiled=True),
            lax.psum_scatter(grad_enc_out, "dp", scatter_dimension=1, tiled=True),
            lax.psum_scatter(grad_enc_up, "dp", scatter_dimension=0, tiled=True),
            lax.psum_scatter(grad_enc_down, "dp", scatter_dimension=1, tiled=True),
            lax.psum_scatter(grad_cross_qkv, "dp", scatter_dimension=1, tiled=True),
            lax.psum_scatter(grad_cross_out, "dp", scatter_dimension=1, tiled=True),
            lax.psum_scatter(grad_dec_qkv, "dp", scatter_dimension=1, tiled=True),
            lax.psum_scatter(grad_dec_out, "dp", scatter_dimension=1, tiled=True),
            lax.psum_scatter(grad_dec_up, "dp", scatter_dimension=0, tiled=True),
            lax.psum_scatter(grad_dec_down, "dp", scatter_dimension=1, tiled=True),
            lax.psum_scatter(grad_norms, "dp", scatter_dimension=2, tiled=True),
        )
    )
    return (decoded, grad_mel, grad_embedding) + all_parts + (rms_stats,)


def solution(mesh):
    placed = (
        P("dp", None),
        P(),
        P(),
        P(),
        P("dp", "mp"),
        P(None, None, ("dp", "mp")),
        P(None, ("dp", "mp"), None),
        P(None, "dp", "mp"),
        P("mp", "dp"),
        P("dp", "mp"),
        P("mp", "dp"),
        P(None, "dp", "mp"),
        P("mp", "dp"),
        P(None, "dp", "mp"),
        P("mp", "dp"),
        P("dp", "mp"),
        P("mp", "dp"),
        P(None, None, "dp"),
        P("dp", None),
    )
    return jax.shard_map(
        body,
        mesh=mesh,
        in_specs=placed,
        out_specs=(
            P("dp", None),
            P("dp", None),
            P("dp", "mp"),
            P(None, None, ("dp", "mp")),
            P(None, ("dp", "mp"), None),
            P(None, "dp", "mp"),
            P("mp", "dp"),
            P("dp", "mp"),
            P("mp", "dp"),
            P(None, "dp", "mp"),
            P("mp", "dp"),
            P(None, "dp", "mp"),
            P("mp", "dp"),
            P("dp", "mp"),
            P("mp", "dp"),
            P(None, None, "dp"),
            P(),
        ),
        check_vma=False,
    )
```

profile of v0, /device:TPU:0, one launch (start us, length us, event | category | flops | bytes accessed | tf_op | source)
XLA Modules:
  0.0 2458.1 jit_solution(10924375323496480957)
XLA Ops:
  8.7 33.4 %all_gather.49 = f32[3,80,192]{1,2,0:T(8,128)S(1)} all-gather(f32[3,80,24]{1,2,0:T(8,128)} %param.24), channel_id=1, replica_groups=mesh['dp'=8,'mp'=4] {'dp'}, dimensions={2}, use_global_device_ids=true | all-gather | bytes 207360 | tf_op jit(solution)/shard_map/all_gather | solution.py:141
  168.9 34.4 %all_gather.52 = f32[192,768]{0,1:T(8,128)} all-gather(f32[192,96]{0,1:T(8,128)S(1)} %copy.130), channel_id=1, replica_groups=mesh['dp'=8,'mp'=4] {'dp'}, dimensions={1}, use_global_device_ids=true | all-gather | bytes 663552 | tf_op jit(solution)/shard_map/all_gather | solution.py:144
  203.3 33.4 %all_gather.46 = f32[6,2,768]{0,1,2:T(2,128)S(1)} all-gather(f32[6,2,96]{0,1,2:T(2,128)S(1)} %copy.120), channel_id=1, replica_groups=mesh['dp'=8,'mp'=4] {'dp'}, dimensions={2}, use_global_device_ids=true | all-gather | bytes 41472 | tf_op jit(solution)/shard_map/all_gather | solution.py:153
  236.6 33.6 %slice_reduce_fusion.1 = (f32[768]{0:T(1024)S(1)}, f32[768]{0:T(1024)}, f32[768]{0:T(1024)S(1)}, f32[768]{0:T(1024)S(1)}, f32[768]{0:T(1024)}, /*index=5*/f32[76...) fusion(f32[6,2,768]{0,1,2:T(2,128)S(1)} %all_gather.46), kind=kLoop, calls=%fused_computation.322 | loop fusion | bytes 73728 | tf_op jit(solution)/shard_map/slice | solution.py:24
  345.6 33.9 %all_gather.48 = f32[192,768]{0,1:T(8,128)} all-gather(f32[192,96]{0,1:T(8,128)S(1)} %copy.125), channel_id=1, replica_groups=mesh['dp'=8,'mp'=4] {'dp'}, dimensions={1}, use_global_device_ids=true | all-gather | bytes 663552 | tf_op jit(solution)/shard_map/all_gather | solution.py:150
  392.5 27.5 %all-reduce.51.cloned.1.call-done = f32[1024,768]{1,0:T(8,128)} async-done(((f32[1024,768]{1,0:T(8,128)}), f32[1024,768]{1,0:T(8,128)}) %all-reduce.51.cloned.1.call-update) | async-done | bytes 3145744 | tf_op jit(solution)/shard_map/psum | solution.py:108
  424.4 49.7 %all-gather.19.cloned.1.call-done = f32[768,768]{1,0:T(8,128)} async-done(((f32[96,768]{1,0:T(8,128)}), f32[768,768]{1,0:T(8,128)}) %all-gather.19.cloned.1.call-update) | async-done | bytes 2359312 | tf_op jit(solution)/shard_map/all_gather | solution.py:145
  492.0 34.7 %all-gather.21.cloned.1.call-done = f32[768,768]{0,1:T(8,128)} async-done(((f32[768,96]{0,1:T(8,128)}), f32[768,768]{0,1:T(8,128)}) %all-gather.21.cloned.1.call-update) | async-done | bytes 2359312 | tf_op jit(solution)/shard_map/all_gather | solution.py:146
  561.7 34.5 %all_gather.56 = f32[192,768]{0,1:T(8,128)S(1)} all-gather(f32[192,96]{0,1:T(8,128)S(1)} %copy.134), channel_id=1, replica_groups=mesh['dp'=8,'mp'=4] {'dp'}, dimensions={1}, use_global_device_ids=true | all-gather | bytes 663552 | tf_op jit(solution)/shard_map/all_gather | solution.py:148
  614.8 82.0 %all-reduce.67.cloned.1.call-done = (f32[384,768]{1,0:T(8,128)}, f32[1024,768]{1,0:T(8,128)}) async-done(((f32[384,768]{1,0:T(8,128)}, f32[1024,768]{1,0:T(8,128)}), (f32[384,768]{1,0:T(8,128)}, f32[1024,768]{1,0:T(8,128)})) %all-reduce.67.cloned.1.call-update) | async-done | bytes 4325392 | tf_op jit(solution)/shard_map/psum | solution.py:108
  755.6 34.5 %all-reduce.53.cloned.1.call-done = f32[384,768]{1,0:T(8,128)} async-done(((f32[384,768]{1,0:T(8,128)}), f32[384,768]{1,0:T(8,128)}) %all-reduce.53.cloned.1.call-update) | async-done | bytes 1179664 | tf_op jit(solution)/shard_map/psum | solution.py:108
  794.0 50.1 %all-gather.25.cloned.1.call-done = f32[768,768]{1,0:T(8,128)} async-done(((f32[96,768]{1,0:T(8,128)}), f32[768,768]{1,0:T(8,128)}) %all-gather.25.cloned.1.call-update) | async-done | bytes 2359312 | tf_op jit(solution)/shard_map/all_gather | solution.py:151
  858.0 36.2 %all-reduce.55.cloned.1.call-done = f32[384,768]{1,0:T(8,128)} async-done(((f32[384,768]{1,0:T(8,128)}), f32[384,768]{1,0:T(8,128)}) %all-reduce.55.cloned.1.call-update) | async-done | bytes 1179664 | tf_op jit(solution)/shard_map/psum | solution.py:112
  930.7 68.0 %all-reduce.57.cloned.1.call-done = f32[1024,768]{1,0:T(8,128)} async-done(((f32[1024,768]{1,0:T(8,128)}), f32[1024,768]{1,0:T(8,128)}) %all-reduce.57.cloned.1.call-update) | async-done | bytes 3145744 | tf_op jit(solution)/shard_map/psum | solution.py:112
  1041.5 54.6 %all-reduce.59.cloned.1.call-done = f32[1024,768]{1,0:T(8,128)} async-done(((f32[1024,768]{1,0:T(8,128)}), f32[1024,768]{1,0:T(8,128)}) %all-reduce.59.cloned.1.call-update) | async-done | bytes 3145744 | tf_op jit(solution)/shard_map/psum | solution.py:112
  1186.2 79.2 %all-reduce.65.cloned.1.call-done = (f32[1024,768]{1,0:T(8,128)}, f32[384,768]{1,0:T(8,128)}) async-done(((f32[1024,768]{1,0:T(8,128)}, f32[384,768]{1,0:T(8,128)}), (f32[1024,768]{1,0:T(8,128)}, f32[384,768]{1,0:T(8,128)})) %all-reduce.65.cloned.1.call-update) | async-done | bytes 4325392 | tf_op jit(solution)/shard_map/psum | solution.py:112
  1290.4 31.0 %pad.155 = f32[2048,192]{0,1:T(8,128)} pad(f32[1024,192]{0,1:T(8,128)} %fusion.161, f32[]{:T(128)} %constant.55.clone.1), padding=1_0_1x0_0_0 | pad | bytes 2359300 | tf_op jit(solution)/shard_map/transpose(jvp(jit(_pad)))/pad | solution.py:95
  1327.2 30.9 %pad.156 = f32[2048,192]{0,1:T(8,128)} pad(f32[1024,192]{0,1:T(8,128)} %fusion.159, f32[]{:T(128)} %constant.55.clone.1), padding=0_1_1x0_0_0 | pad | bytes 2359300 | tf_op jit(solution)/shard_map/transpose(jvp(jit(_pad)))/pad | solution.py:95
  1363.8 30.9 %pad.203 = f32[2049,192]{0,1:T(8,128)} pad(f32[1024,192]{0,1:T(8,128)} %fusion.157, f32[]{:T(128)} %constant.55.clone.1), padding=0_2_1x0_0_0 | pad | bytes 2360068
  1583.1 34.6 %reduce-scatter.44.cloned.1.call-done = f32[96,576]{1,0:T(8,128)} async-done(((f32[768,576]{1,0:T(8,128)}), f32[96,576]{1,0:T(8,128)}) %reduce-scatter.44.cloned.1.call-update) | async-done | bytes 221200
  1621.4 61.9 %reduce-scatter.42.cloned.1.call-done = f32[96,192]{1,0:T(8,128)} async-done(((f32[768,192]{1,0:T(8,128)}), f32[96,192]{1,0:T(8,128)}) %reduce-scatter.42.cloned.1.call-update) | async-done | bytes 73744
  1684.9 63.0 %reduce-scatter.52.cloned.1.call-done = f32[96,12]{1,0:T(8,128)} async-done(((f32[768,12]{1,0:T(8,128)}), f32[96,12]{1,0:T(8,128)}) %reduce-scatter.52.cloned.1.call-update) | async-done | bytes 4624
  1751.3 70.6 %all-reduce.61.cloned.1.call-done = f32[3,80,192]{1,0,2:T(4,128)} async-done(((f32[3,80,192]{1,0,2:T(4,128)}), f32[3,80,192]{1,0,2:T(4,128)}) %all-reduce.61.cloned.1.call-update) | async-done | bytes 184336
  1823.3 64.2 %reduce-scatter.50.cloned.1.call-done = f32[96,192]{1,0:T(8,128)} async-done(((f32[768,192]{1,0:T(8,128)}), f32[96,192]{1,0:T(8,128)}) %reduce-scatter.50.cloned.1.call-update) | async-done | bytes 73744
  1889.2 68.3 %reduce-scatter.40.cloned.1.call-done = f32[96,576]{1,0:T(8,128)} async-done(((f32[768,576]{1,0:T(8,128)}), f32[96,576]{1,0:T(8,128)}) %reduce-scatter.40.cloned.1.call-update) | async-done | bytes 221200
  1991.5 35.7 %reduce-scatter.48.cloned.1.call-done = f32[96,576]{1,0:T(8,128)} async-done(((f32[768,576]{1,0:T(8,128)}), f32[96,576]{1,0:T(8,128)}) %reduce-scatter.48.cloned.1.call-update) | async-done | bytes 221200
  2029.1 59.7 %all-gather.29.cloned.1.call-done = f32[3072,192]{1,0:T(8,128)} async-done(((f32[384,192]{1,0:T(8,128)}), f32[3072,192]{1,0:T(8,128)}) %all-gather.29.cloned.1.call-update) | async-done | bytes 2359312 | tf_op jit(solution)/shard_map/all_gather | solution.py:292
  2120.7 40.6 %reduce-scatter.38.cloned.1.call-done = f32[768,96]{0,1:T(8,128)} async-done(((f32[768,768]{0,1:T(8,128)}), f32[768,96]{0,1:T(8,128)}) %reduce-scatter.38.cloned.1.call-update) | async-done | bytes 294928 | tf_op jit(solution)/shard_map/reduce_scatter | solution.py:350
  2161.3 72.9 %reduce-scatter.36.cloned.1.call-done = f32[96,768]{1,0:T(8,128)} async-done(((f32[768,768]{1,0:T(8,128)}), f32[96,768]{1,0:T(8,128)}) %reduce-scatter.36.cloned.1.call-update) | async-done | bytes 294928 | tf_op jit(solution)/shard_map/reduce_scatter | solution.py:349
  2234.2 73.1 %reduce-scatter.34.cloned.1.call-done = f32[768,96]{0,1:T(8,128)} async-done(((f32[768,768]{0,1:T(8,128)}), f32[768,96]{0,1:T(8,128)}) %reduce-scatter.34.cloned.1.call-update) | async-done | bytes 294928 | tf_op jit(solution)/shard_map/reduce_scatter | solution.py:344
  2307.3 73.1 %reduce-scatter.32.cloned.1.call-done = f32[96,768]{1,0:T(8,128)} async-done(((f32[768,768]{1,0:T(8,128)}), f32[96,768]{1,0:T(8,128)}) %reduce-scatter.32.cloned.1.call-update) | async-done | bytes 294928 | tf_op jit(solution)/shard_map/reduce_scatter | solution.py:343
  2380.4 69.6 %reduce-scatter.30.cloned.1.call-done = f32[3,24,768]{2,1,0:T(8,128)} async-done(((f32[3,192,768]{2,1,0:T(8,128)}), f32[3,24,768]{2,1,0:T(8,128)}) %reduce-scatter.30.cloned.1.call-update) | async-done | bytes 221200 | tf_op jit(solution)/shard_map/reduce_scatter | solution.py:340
  (772 shorter events, 838.8 us)
Async XLA Ops:
  7.2 125.6 %all-gather.15.cloned.1.call-start = ((), (), s32[]{:S(2)}) async-start(), calls=%async_computation.16 | async-start | bytes 1990656 | tf_op jit(solution)/shard_map/all_gather | solution.py:142
  7.9 270.1 %all-gather.17.cloned.1.call-start = ((), (), s32[]{:S(2)}) async-start(), calls=%async_computation.18 | async-start | bytes 2654208 | tf_op jit(solution)/shard_map/all_gather | solution.py:143
  8.7 274.3 %all-reduce.49.cloned.1.call-start = ((), (), s32[]{:S(2)}) async-start(), calls=%async_computation.17 | async-start | bytes 6291456 | tf_op jit(solution)/shard_map/psum | solution.py:108
  145.0 197.1 %reduce-scatter.28.cloned.1.call-start = ((), (), s32[]{:S(2)}) async-start(), calls=%async_computation.13 | async-start | bytes 3538944 | tf_op jit(solution)/shard_map/reduce_scatter | solution.py:198
  167.7 215.0 %all-gather.13.cloned.1.call-start = ((), (), s32[]{:S(2)}) async-start(), calls=%async_computation.15 | async-start | bytes 2654208 | tf_op jit(solution)/shard_map/all_gather | solution.py:149
  168.3 251.6 %all-reduce.51.cloned.1.call-start = ((), (), s32[]{:S(2)}) async-start(), calls=%async_computation.19 | async-start | bytes 6291456 | tf_op jit(solution)/shard_map/psum | solution.py:108
  340.5 133.6 %all-gather.19.cloned.1.call-start = ((), (), s32[]{:S(2)}) async-start(), calls=%async_computation.20 | async-start | bytes 2654208 | tf_op jit(solution)/shard_map/all_gather | solution.py:145
  341.2 185.4 %all-gather.21.cloned.1.call-start = ((), (), s32[]{:S(2)}) async-start(), calls=%async_computation.21 | async-start | bytes 2654208 | tf_op jit(solution)/shard_map/all_gather | solution.py:146
  342.0 202.8 %all-gather.11.cloned.1.call-start = ((), (), s32[]{:S(2)}) async-start(), calls=%async_computation.14 | async-start | bytes 1474560 | tf_op jit(solution)/shard_map/all_gather | solution.py:201
  343.9 262.5 %all-gather.23.cloned.1.call-start = ((), (), s32[]{:S(2)}) async-start(), calls=%async_computation.22 | async-start | bytes 2654208 | tf_op jit(solution)/shard_map/all_gather | solution.py:147
  344.5 352.3 %all-reduce.67.cloned.1.call-start = ((), (), s32[]{:S(2)}) async-start(), calls=%async_computation.45 | async-start | bytes 8650752 | tf_op jit(solution)/shard_map/psum | solution.py:108
  560.8 190.1 %all-gather.27.cloned.1.call-start = ((), (), s32[]{:S(2)}) async-start(), calls=%async_computation.25 | async-start | bytes 2654208 | tf_op jit(solution)/shard_map/all_gather | solution.py:152
  561.4 228.8 %all-reduce.53.cloned.1.call-start = ((), (), s32[]{:S(2)}) async-start(), calls=%async_computation.23 | async-start | bytes 2359296 | tf_op jit(solution)/shard_map/psum | solution.py:108
  731.6 162.5 %all-reduce.55.cloned.1.call-start = ((), (), s32[]{:S(2)}) async-start(), calls=%async_computation.26 | async-start | bytes 2359296 | tf_op jit(solution)/shard_map/psum | solution.py:112
  857.9 140.8 %all-reduce.57.cloned.1.call-start = ((), (), s32[]{:S(2)}) async-start(), calls=%async_computation.27 | async-start | bytes 6291456 | tf_op jit(solution)/shard_map/psum | solution.py:112
  930.0 166.2 %all-reduce.59.cloned.1.call-start = ((), (), s32[]{:S(2)}) async-start(), calls=%async_computation.28 | async-start | bytes 6291456 | tf_op jit(solution)/shard_map/psum | solution.py:112
  1027.5 237.9 %all-reduce.65.cloned.1.call-start = ((), (), s32[]{:S(2)}) async-start(), calls=%async_computation.44 | async-start | bytes 8650752 | tf_op jit(solution)/shard_map/psum | solution.py:112
  1177.5 344.1 %all-reduce.63.cloned.1.call-start = ((), (), s32[]{:S(2)}) async-start(), calls=%async_computation.43 | async-start | bytes 6029312 | tf_op jit(solution)/shard_map/psum | solution.py:108
  1414.3 167.2 %reduce-scatter.46.cloned.1.call-start = ((), (), s32[]{:S(2)}) async-start(), calls=%async_computation.38 | async-start | bytes 884736
  1418.9 198.8 %reduce-scatter.44.cloned.1.call-start = ((), (), s32[]{:S(2)}) async-start(), calls=%async_computation.37 | async-start | bytes 2211840
  1440.9 242.4 %reduce-scatter.42.cloned.1.call-start = ((), (), s32[]{:S(2)}) async-start(), calls=%async_computation.36 | async-start | bytes 884736
  1449.4 298.4 %reduce-scatter.52.cloned.1.call-start = ((), (), s32[]{:S(2)}) async-start(), calls=%async_computation.41 | async-start | bytes 442368
  1474.4 347.5 %all-reduce.61.cloned.1.call-start = ((), (), s32[]{:S(2)}) async-start(), calls=%async_computation.42 | async-start | bytes 786432
  1478.0 409.6 %reduce-scatter.50.cloned.1.call-start = ((), (), s32[]{:S(2)}) async-start(), calls=%async_computation.40 | async-start | bytes 884736
  1482.4 475.0 %reduce-scatter.40.cloned.1.call-start = ((), (), s32[]{:S(2)}) async-start(), calls=%async_computation.35 | async-start | bytes 2211840
  1504.1 523.1 %reduce-scatter.48.cloned.1.call-start = ((), (), s32[]{:S(2)}) async-start(), calls=%async_computation.39 | async-start | bytes 2211840
  1521.6 567.3 %all-gather.29.cloned.1.call-start = ((), (), s32[]{:S(2)}) async-start(), calls=%async_computation.29 | async-start | bytes 3538944 | tf_op jit(solution)/shard_map/all_gather | solution.py:292
  1523.9 637.3 %reduce-scatter.38.cloned.1.call-start = ((), (), s32[]{:S(2)}) async-start(), calls=%async_computation.34 | async-start | bytes 2654208 | tf_op jit(solution)/shard_map/reduce_scatter | solution.py:350
  1531.5 702.8 %reduce-scatter.36.cloned.1.call-start = ((), (), s32[]{:S(2)}) async-start(), calls=%async_computation.33 | async-start | bytes 2654208 | tf_op jit(solution)/shard_map/reduce_scatter | solution.py:349
  1540.4 766.9 %reduce-scatter.34.cloned.1.call-start = ((), (), s32[]{:S(2)}) async-start(), calls=%async_computation.32 | async-start | bytes 2654208 | tf_op jit(solution)/shard_map/reduce_scatter | solution.py:344
  1552.6 827.8 %reduce-scatter.32.cloned.1.call-start = ((), (), s32[]{:S(2)}) async-start(), calls=%async_computation.31 | async-start | bytes 2654208 | tf_op jit(solution)/shard_map/reduce_scatter | solution.py:343
  1567.4 882.6 %reduce-scatter.30.cloned.1.call-start = ((), (), s32[]{:S(2)}) async-start(), calls=%async_computation.30 | async-start | bytes 1990656 | tf_op jit(solution)/shard_map/reduce_scatter | solution.py:340
  (222 other events, 9723.5 us)
Sparse Core Ops, SparseCore 0:
  10.2 49.2 all-gather.14
  61.7 50.6 all-gather.16
  145.1 69.0 all-reduce.48
  218.2 75.4 reduce-scatter.27
  295.7 55.1 all-gather.12
  353.1 66.8 all-reduce.50
  422.1 51.9 all-gather.18
  476.3 50.3 all-gather.20
  546.8 59.5 all-gather.22
  609.5 87.3 all-reduce.66
  698.8 51.9 all-gather.26
  753.8 36.2 all-reduce.52
  792.2 51.9 all-gather.24
  858.0 36.0 all-reduce.54
  930.1 68.5 all-reduce.56
  1027.6 68.5 all-reduce.58
  1177.6 87.7 all-reduce.64
  1414.4 66.8 all-reduce.62
  1484.4 63.3 reduce-scatter.45
  1551.3 66.4 reduce-scatter.43
  1621.0 62.1 reduce-scatter.41
  1686.5 61.2 reduce-scatter.51
  1751.1 70.7 all-reduce.60
  1825.2 62.2 reduce-scatter.49
  1890.9 66.5 reduce-scatter.39
  1960.8 66.4 reduce-scatter.47
  2030.0 58.8 all-gather.28
  2092.9 68.3 reduce-scatter.37
  2165.2 68.9 reduce-scatter.35
  2238.3 68.9 reduce-scatter.33
  2311.4 68.9 reduce-scatter.31
  2384.3 65.6 reduce-scatter.29
  (1 shorter events, 15.9 us)
where the time goes:
time: 2470 us; the launch traced here: 2460 us
  waiting for transfers between devices  1340 us (54%)
  matrix products  430 us (17%)
  local copies, waits for them, and re-layouts  334 us (14%)
  blocking collectives  200 us (8%)
  other arithmetic  126 us (5%)
    unnamed x41, waiting for transfers between devices  404 us
    dot_general x63, matrix products, matmul(): jnp.dot(left, right, precision=HIGH, preferred_element_type=jnp.float32)  296 us
    psum x4, waiting for transfers between devices, input_sum(): return lax.psum((grad_rows, grad_norm), 'mp')  238 us
    psum x5, waiting for transfers between devices, branch_sum(): return lax.psum(tensor, 'mp')  144 us
    unnamed x478, local copies, waits for them, and re-layouts  111 us
    reduce_scatter x1, waiting for transfers between devices, body(): lax.psum_scatter(grad_enc_down, 'dp', scatter_dimension=1, tiled=True)  73.1 us
    reduce_scatter x1, waiting for transfers between devices, body(): lax.psum_scatter(grad_enc_up, 'dp', scatter_dimension=0, tiled=True)  73.1 us
    reduce_scatter x1, waiting for transfers between devices, body(): lax.psum_scatter(grad_dec_up, 'dp', scatter_dimension=0, tiled=True)  72.9 us
  transfers between devices with their start and end apart: 33, of which 26 were waited for; matrix products, arithmetic and copies ran while one was open for 23% of the time, Pallas kernels for 0%

commit v1 on v0

--- a/solution.py
+++ b/solution.py
@@ -105,7 +105,7 @@
 
 
 def branch_sum(tensor):
-    return lax.psum(tensor, "mp")
+    return jnp.sum(lax.all_gather(tensor, "mp"), axis=0)
 
 
 def input_sum(grad_rows, grad_norm):

time: 2470 us -> 2430 us (0.984)
  waiting for transfers between devices: 1340 us -> 1270 us
  other arithmetic: 126 us -> 160 us
    all_gather x0 -> x7, waiting for transfers between devices: none -> 221 us  [branch_sum(): return jnp.sum(lax.all_gather(tensor, 'mp'), axis=0)]
    psum x5 -> x0, waiting for transfers between devices: 144 us -> none  [branch_sum(): return lax.psum(tensor, 'mp')]
    unnamed x41 -> x43, waiting for transfers between devices: 404 us -> 280 us
    reduce_sum x0 -> x7, other arithmetic: none -> 33.9 us  [branch_sum(): return jnp.sum(lax.all_gather(tensor, 'mp'), axis=0)]
    reduce_scatter x1, waiting for transfers between devices: 40.6 us -> 73.1 us  [body(): lax.psum_scatter(grad_dec_down, 'dp', scatter_dimension=1, tiled=True)]
    reduce_scatter x1, waiting for transfers between devices: 72.9 us -> 40.6 us  [body(): lax.psum_scatter(grad_dec_up, 'dp', scatter_dimension=0, tiled=True)]
    psum x4, waiting for transfers between devices: 238 us -> 210 us  [input_sum(): return lax.psum((grad_rows, grad_norm), 'mp')]
    all_gather x1, waiting for transfers between devices: 18.8 us -> 43.9 us  [body(): lax.all_gather(dec_down, 'dp', axis=1, tiled=True)]
  transfers between devices with their start and end apart: 33 -> 35, of which waited for: 26 -> 26; matrix products, arithmetic and copies ran while one was open for 23% -> 28% of each run, Pallas kernels for 0% -> 0%
where the time goes in v1:
time: 2430 us
  waiting for transfers between devices  1270 us (52%)
  matrix products  443 us (18%)
  local copies, waits for them, and re-layouts  325 us (13%)
  blocking collectives  204 us (8%)
  other arithmetic  160 us (7%)
    dot_general x63, matrix products, matmul(): jnp.dot(left, right, precision=HIGH, preferred_element_type=jnp.float32)  309 us
    unnamed x43, waiting for transfers between devices  280 us
    all_gather x7, waiting for transfers between devices, branch_sum(): return jnp.sum(lax.all_gather(tensor, 'mp'), axis=0)  221 us
    psum x4, waiting for transfers between devices, input_sum(): return lax.psum((grad_rows, grad_norm), 'mp')  210 us
    unnamed x463, local copies, waits for them, and re-layouts  106 us
    reduce_scatter x1, waiting for transfers between devices, body(): lax.psum_scatter(grad_dec_down, 'dp', scatter_dimension=1, tiled=True)  73.1 us
    reduce_scatter x1, waiting for transfers between devices, body(): lax.psum_scatter(grad_enc_down, 'dp', scatter_dimension=1, tiled=True)  72.9 us
    reduce_scatter x1, waiting for transfers between devices, body(): lax.psum_scatter(grad_enc_up, 'dp', scatter_dimension=0, tiled=True)  72.8 us
  transfers between devices with their start and end apart: 35, of which 26 were waited for; matrix products, arithmetic and copies ran while one was open for 28% of the time, Pallas kernels for 0%

profile of v1, /device:TPU:0, one launch (start us, length us, event | category | flops | bytes accessed | tf_op | source)
XLA Modules:
  0.0 2426.0 jit_solution(14492148486295312881)
XLA Ops:
  33.5 33.6 %all_gather.93 = f32[3,80,192]{1,2,0:T(8,128)S(1)} all-gather(f32[3,80,24]{1,2,0:T(8,128)S(1)} %copy-done.159), channel_id=1, replica_groups=mesh['dp'=8,'mp'=4] {'dp'}, dimensions={2}, use_global_device_ids=true | all-gather | bytes 207360 | tf_op jit(solution)/shard_map/all_gather | solution.py:141
  77.0 26.3 %slice.178 = f32[1024,192]{0,1:T(8,128)S(1)} slice(f32[2050,192]{0,1:T(8,128)S(1)} %pad.114), slice={[0:2048:2], [0:192:1]} | slice | bytes 1572864 | tf_op jit(solution)/shard_map/slice | solution.py:97
  129.7 27.1 %slice.182 = f32[1024,192]{0,1:T(8,128)} slice(f32[2050,192]{0,1:T(8,128)S(1)} %pad.114), slice={[2:2050:2], [0:192:1]} | slice | bytes 1572864 | tf_op jit(solution)/shard_map/slice | solution.py:99
  170.6 33.9 %all_gather.88 = f32[6,2,768]{0,1,2:T(2,128)S(1)} all-gather(f32[6,2,96]{0,1,2:T(2,128)S(1)} %copy.120), channel_id=1, replica_groups=mesh['dp'=8,'mp'=4] {'dp'}, dimensions={2}, use_global_device_ids=true | all-gather | bytes 41472 | tf_op jit(solution)/shard_map/all_gather | solution.py:153
  204.5 33.8 %all_gather.98 = f32[192,768]{0,1:T(8,128)} all-gather(f32[192,96]{0,1:T(8,128)S(1)} %copy.130), channel_id=1, replica_groups=mesh['dp'=8,'mp'=4] {'dp'}, dimensions={1}, use_global_device_ids=true | all-gather | bytes 663552 | tf_op jit(solution)/shard_map/all_gather | solution.py:144
  245.7 33.4 %slice_reduce_fusion.1 = (f32[768]{0:T(1024)}, f32[768]{0:T(1024)}, f32[768]{0:T(1024)}, f32[768]{0:T(1024)S(1)}, f32[768]{0:T(1024)}, /*index=5*/f32[768]{0:T(1...) fusion(f32[6,2,768]{0,1,2:T(2,128)S(1)} %all_gather.88), kind=kLoop, calls=%fused_computation.322 | loop fusion | bytes 73728 | tf_op jit(solution)/shard_map/slice | solution.py:24
  356.6 32.0 %all_gather.90 = f32[192,768]{0,1:T(8,128)S(1)} all-gather(f32[192,96]{0,1:T(8,128)S(1)} %copy.125), channel_id=1, replica_groups=mesh['dp'=8,'mp'=4] {'dp'}, dimensions={1}, use_global_device_ids=true | all-gather | bytes 663552 | tf_op jit(solution)/shard_map/all_gather | solution.py:150
  448.5 41.0 %all-gather.33.cloned.1.call-done = f32[768,768]{1,0:T(8,128)} async-done(((f32[96,768]{1,0:T(8,128)}), f32[768,768]{1,0:T(8,128)}) %all-gather.33.cloned.1.call-update) | async-done | bytes 2359312 | tf_op jit(solution)/shard_map/all_gather | solution.py:145
  507.8 34.2 %all-gather.35.cloned.1.call-done = f32[768,768]{0,1:T(8,128)} async-done(((f32[768,96]{0,1:T(8,128)}), f32[768,768]{0,1:T(8,128)}) %all-gather.35.cloned.1.call-update) | async-done | bytes 2359312 | tf_op jit(solution)/shard_map/all_gather | solution.py:146
  554.8 36.2 %all_gather.106 = f32[192,768]{0,1:T(8,128)} all-gather(f32[192,96]{0,1:T(8,128)S(1)} %copy.134), channel_id=1, replica_groups=mesh['dp'=8,'mp'=4] {'dp'}, dimensions={1}, use_global_device_ids=true | all-gather | bytes 663552 | tf_op jit(solution)/shard_map/all_gather | solution.py:148
  605.7 34.4 %all-gather.45.cloned.1.call-done = f32[1536,768]{1,0:T(8,128)} async-done(((f32[384,768]{1,0:T(8,128)}), f32[1536,768]{1,0:T(8,128)}) %all-gather.45.cloned.1.call-update) | async-done | bytes 4718608 | tf_op jit(solution)/shard_map/all_gather | solution.py:108
  646.3 77.4 %all-gather.51.cloned.1.call-done = f32[4096,768]{1,0:T(8,128)} async-done(((f32[1024,768]{1,0:T(8,128)}), f32[4096,768]{1,0:T(8,128)}) %all-gather.51.cloned.1.call-update) | async-done | bytes 12582928 | tf_op jit(solution)/shard_map/all_gather | solution.py:108
  763.8 36.4 %all-gather.53.cloned.1.call-done = f32[1536,768]{1,0:T(8,128)} async-done(((f32[384,768]{1,0:T(8,128)}), f32[1536,768]{1,0:T(8,128)}) %all-gather.53.cloned.1.call-update) | async-done | bytes 4718608 | tf_op jit(solution)/shard_map/all_gather | solution.py:108
  808.0 46.1 %all-gather.39.cloned.1.call-done = f32[768,768]{1,0:T(8,128)} async-done(((f32[96,768]{1,0:T(8,128)}), f32[768,768]{1,0:T(8,128)}) %all-gather.39.cloned.1.call-update) | async-done | bytes 2359312 | tf_op jit(solution)/shard_map/all_gather | solution.py:151
  862.6 43.9 %all-gather.41.cloned.1.call-done = f32[768,768]{0,1:T(8,128)} async-done(((f32[768,96]{0,1:T(8,128)}), f32[768,768]{0,1:T(8,128)}) %all-gather.41.cloned.1.call-update) | async-done | bytes 2359312 | tf_op jit(solution)/shard_map/all_gather | solution.py:152
  959.8 36.8 %all-reduce.43.cloned.1.call-done = f32[384,768]{1,0:T(8,128)} async-done(((f32[384,768]{1,0:T(8,128)}), f32[384,768]{1,0:T(8,128)}) %all-reduce.43.cloned.1.call-update) | async-done | bytes 1179664 | tf_op jit(solution)/shard_map/psum | solution.py:112
  1060.6 55.5 %all-reduce.45.cloned.1.call-done = f32[1024,768]{1,0:T(8,128)} async-done(((f32[1024,768]{1,0:T(8,128)}), f32[1024,768]{1,0:T(8,128)}) %all-reduce.45.cloned.1.call-update) | async-done | bytes 3145744 | tf_op jit(solution)/shard_map/psum | solution.py:112
  1146.9 85.9 %all-reduce.51.cloned.1.call-done = (f32[1024,768]{1,0:T(8,128)}, f32[384,768]{1,0:T(8,128)}) async-done(((f32[1024,768]{1,0:T(8,128)}, f32[384,768]{1,0:T(8,128)}), (f32[1024,768]{1,0:T(8,128)}, f32[384,768]{1,0:T(8,128)})) %all-reduce.51.cloned.1.call-update) | async-done | bytes 4325392 | tf_op jit(solution)/shard_map/psum | solution.py:112
  1390.4 31.6 %all-reduce.49.cloned.1.call-done = (f32[1024,768]{1,0:T(8,128)}, f32[384,768]{1,0:T(8,128)}) async-done(((f32[1024,768]{1,0:T(8,128)}, f32[384,768]{1,0:T(8,128)}), (f32[1024,768]{1,0:T(8,128)}, f32[384,768]{1,0:T(8,128)})) %all-reduce.49.cloned.1.call-update) | async-done | bytes 4325392 | tf_op jit(solution)/shard_map/psum | solution.py:112
  1436.4 31.1 %pad.203 = f32[2049,192]{0,1:T(8,128)} pad(f32[1024,192]{0,1:T(8,128)} %fusion.157, f32[]{:T(128)} %constant.55.clone.1), padding=0_2_1x0_0_0 | pad | bytes 2360068
  1473.0 31.2 %pad.156 = f32[2048,192]{0,1:T(8,128)} pad(f32[1024,192]{0,1:T(8,128)} %fusion.159, f32[]{:T(128)} %constant.55.clone.1), padding=0_1_1x0_0_0 | pad | bytes 2359300 | tf_op jit(solution)/shard_map/transpose(jvp(jit(_pad)))/pad | solution.py:95
  1509.8 31.0 %pad.155 = f32[2048,192]{0,1:T(8,128)} pad(f32[1024,192]{0,1:T(8,128)} %fusion.161, f32[]{:T(128)} %constant.55.clone.1), padding=1_0_1x0_0_0 | pad | bytes 2359300 | tf_op jit(solution)/shard_map/transpose(jvp(jit(_pad)))/pad | solution.py:95
  1690.5 64.0 %reduce-scatter.50.cloned.1.call-done = f32[96,192]{1,0:T(8,128)} async-done(((f32[768,192]{1,0:T(8,128)}), f32[96,192]{1,0:T(8,128)}) %reduce-scatter.50.cloned.1.call-update) | async-done | bytes 73744
  1756.1 72.4 %all-reduce.47.cloned.1.call-done = f32[3,80,192]{1,0,2:T(4,128)} async-done(((f32[3,80,192]{1,0,2:T(4,128)}), f32[3,80,192]{1,0,2:T(4,128)}) %all-reduce.47.cloned.1.call-update) | async-done | bytes 184336
  1830.0 68.5 %reduce-scatter.48.cloned.1.call-done = f32[96,576]{1,0:T(8,128)} async-done(((f32[768,576]{1,0:T(8,128)}), f32[96,576]{1,0:T(8,128)}) %reduce-scatter.48.cloned.1.call-update) | async-done | bytes 221200
  1900.4 68.3 %reduce-scatter.40.cloned.1.call-done = f32[96,576]{1,0:T(8,128)} async-done(((f32[768,576]{1,0:T(8,128)}), f32[96,576]{1,0:T(8,128)}) %reduce-scatter.40.cloned.1.call-update) | async-done | bytes 221200
  2001.3 56.6 %all-gather.43.cloned.1.call-done = f32[3072,192]{1,0:T(8,128)} async-done(((f32[384,192]{1,0:T(8,128)}), f32[3072,192]{1,0:T(8,128)}) %all-gather.43.cloned.1.call-update) | async-done | bytes 2359312 | tf_op jit(solution)/shard_map/all_gather | solution.py:292
  2089.7 40.6 %reduce-scatter.36.cloned.1.call-done = f32[96,768]{1,0:T(8,128)} async-done(((f32[768,768]{1,0:T(8,128)}), f32[96,768]{1,0:T(8,128)}) %reduce-scatter.36.cloned.1.call-update) | async-done | bytes 294928 | tf_op jit(solution)/shard_map/reduce_scatter | solution.py:349
  2130.3 73.1 %reduce-scatter.38.cloned.1.call-done = f32[768,96]{0,1:T(8,128)} async-done(((f32[768,768]{0,1:T(8,128)}), f32[768,96]{0,1:T(8,128)}) %reduce-scatter.38.cloned.1.call-update) | async-done | bytes 294928 | tf_op jit(solution)/shard_map/reduce_scatter | solution.py:350
  2203.4 72.9 %reduce-scatter.34.cloned.1.call-done = f32[768,96]{0,1:T(8,128)} async-done(((f32[768,768]{0,1:T(8,128)}), f32[768,96]{0,1:T(8,128)}) %reduce-scatter.34.cloned.1.call-update) | async-done | bytes 294928 | tf_op jit(solution)/shard_map/reduce_scatter | solution.py:344
  2276.4 72.8 %reduce-scatter.32.cloned.1.call-done = f32[96,768]{1,0:T(8,128)} async-done(((f32[768,768]{1,0:T(8,128)}), f32[96,768]{1,0:T(8,128)}) %reduce-scatter.32.cloned.1.call-update) | async-done | bytes 294928 | tf_op jit(solution)/shard_map/reduce_scatter | solution.py:343
  2349.2 70.1 %reduce-scatter.30.cloned.1.call-done = f32[3,24,768]{2,1,0:T(8,128)} async-done(((f32[3,192,768]{2,1,0:T(8,128)}), f32[3,24,768]{2,1,0:T(8,128)}) %reduce-scatter.30.cloned.1.call-update) | async-done | bytes 221200 | tf_op jit(solution)/shard_map/reduce_scatter | solution.py:340
  (769 shorter events, 875.3 us)
Async XLA Ops:
  7.2 149.6 %all-gather.29.cloned.1.call-start = ((), (), s32[]{:S(2)}) async-start(), calls=%async_computation.16 | async-start | bytes 1990656 | tf_op jit(solution)/shard_map/all_gather | solution.py:142
  7.9 271.2 %all-gather.31.cloned.1.call-start = ((), (), s32[]{:S(2)}) async-start(), calls=%async_computation.17 | async-start | bytes 2654208 | tf_op jit(solution)/shard_map/all_gather | solution.py:143
  8.7 275.4 %reduce-scatter.28.cloned.1.call-start = ((), (), s32[]{:S(2)}) async-start(), calls=%async_computation.13 | async-start | bytes 3538944 | tf_op jit(solution)/shard_map/reduce_scatter | solution.py:198
  32.8 253.3 %all-gather.47.cloned.1.call-start = ((), (), s32[]{:S(2)}) async-start(), calls=%async_computation.32 | async-start | bytes 15728640 | tf_op jit(solution)/shard_map/all_gather | solution.py:108
  168.8 219.8 %all-gather.27.cloned.1.call-start = ((), (), s32[]{:S(2)}) async-start(), calls=%async_computation.15 | async-start | bytes 2654208 | tf_op jit(solution)/shard_map/all_gather | solution.py:149
  169.4 224.5 %all-gather.25.cloned.1.call-start = ((), (), s32[]{:S(2)}) async-start(), calls=%async_computation.14 | async-start | bytes 1474560 | tf_op jit(solution)/shard_map/all_gather | solution.py:201
  286.0 149.5 %all-gather.49.cloned.1.call-start = ((), (), s32[]{:S(2)}) async-start(), calls=%async_computation.33 | async-start | bytes 15728640 | tf_op jit(solution)/shard_map/all_gather | solution.py:108
  350.3 191.7 %all-gather.35.cloned.1.call-start = ((), (), s32[]{:S(2)}) async-start(), calls=%async_computation.19 | async-start | bytes 2654208 | tf_op jit(solution)/shard_map/all_gather | solution.py:146
  351.1 249.7 %all-gather.37.cloned.1.call-start = ((), (), s32[]{:S(2)}) async-start(), calls=%async_computation.20 | async-start | bytes 2654208 | tf_op jit(solution)/shard_map/all_gather | solution.py:147
  351.6 288.5 %all-gather.45.cloned.1.call-start = ((), (), s32[]{:S(2)}) async-start(), calls=%async_computation.31 | async-start | bytes 5898240 | tf_op jit(solution)/shard_map/all_gather | solution.py:108
  409.9 313.8 %all-gather.51.cloned.1.call-start = ((), (), s32[]{:S(2)}) async-start(), calls=%async_computation.34 | async-start | bytes 15728640 | tf_op jit(solution)/shard_map/all_gather | solution.py:108
  553.8 246.4 %all-gather.53.cloned.1.call-start = ((), (), s32[]{:S(2)}) async-start(), calls=%async_computation.35 | async-start | bytes 5898240 | tf_op jit(solution)/shard_map/all_gather | solution.py:108
  763.2 143.3 %all-gather.41.cloned.1.call-start = ((), (), s32[]{:S(2)}) async-start(), calls=%async_computation.22 | async-start | bytes 2654208 | tf_op jit(solution)/shard_map/all_gather | solution.py:152
  763.8 185.4 %all-gather.55.cloned.1.call-start = ((), (), s32[]{:S(2)}) async-start(), calls=%async_computation.36 | async-start | bytes 5898240 | tf_op jit(solution)/shard_map/all_gather | solution.py:108
  959.0 157.1 %all-reduce.45.cloned.1.call-start = ((), (), s32[]{:S(2)}) async-start(), calls=%async_computation.24 | async-start | bytes 6291456 | tf_op jit(solution)/shard_map/psum | solution.py:112
  1047.3 185.4 %all-reduce.51.cloned.1.call-start = ((), (), s32[]{:S(2)}) async-start(), calls=%async_computation.47 | async-start | bytes 8650752 | tf_op jit(solution)/shard_map/psum | solution.py:112
  1144.8 277.2 %all-reduce.49.cloned.1.call-start = ((), (), s32[]{:S(2)}) async-start(), calls=%async_computation.46 | async-start | bytes 8650752 | tf_op jit(solution)/shard_map/psum | solution.py:112
  1333.3 320.0 %reduce-scatter.46.cloned.1.call-start = ((), (), s32[]{:S(2)}) async-start(), calls=%async_computation.41 | async-start | bytes 884736
  1337.3 317.6 %reduce-scatter.44.cloned.1.call-start = ((), (), s32[]{:S(2)}) async-start(), calls=%async_computation.40 | async-start | bytes 2211840
  1355.7 330.2 %reduce-scatter.52.cloned.1.call-start = ((), (), s32[]{:S(2)}) async-start(), calls=%async_computation.44 | async-start | bytes 442368
  1374.5 314.4 %reduce-scatter.42.cloned.1.call-start = ((), (), s32[]{:S(2)}) async-start(), calls=%async_computation.39 | async-start | bytes 884736
  1382.8 371.7 %reduce-scatter.50.cloned.1.call-start = ((), (), s32[]{:S(2)}) async-start(), calls=%async_computation.43 | async-start | bytes 884736
  1390.3 438.2 %all-reduce.47.cloned.1.call-start = ((), (), s32[]{:S(2)}) async-start(), calls=%async_computation.45 | async-start | bytes 786432
  1554.5 344.1 %reduce-scatter.48.cloned.1.call-start = ((), (), s32[]{:S(2)}) async-start(), calls=%async_computation.42 | async-start | bytes 2211840
  1567.6 401.1 %reduce-scatter.40.cloned.1.call-start = ((), (), s32[]{:S(2)}) async-start(), calls=%async_computation.38 | async-start | bytes 2211840
  1589.5 405.7 %all-gather.57.cloned.1.call-start = ((), (), s32[]{:S(2)}) async-start(), calls=%async_computation.37 | async-start | bytes 3276800 | tf_op jit(solution)/shard_map/all_gather | solution.py:108
  1595.7 462.2 %all-gather.43.cloned.1.call-start = ((), (), s32[]{:S(2)}) async-start(), calls=%async_computation.25 | async-start | bytes 3538944 | tf_op jit(solution)/shard_map/all_gather | solution.py:292
  1598.0 532.3 %reduce-scatter.36.cloned.1.call-start = ((), (), s32[]{:S(2)}) async-start(), calls=%async_computation.29 | async-start | bytes 2654208 | tf_op jit(solution)/shard_map/reduce_scatter | solution.py:349
  1606.4 597.0 %reduce-scatter.38.cloned.1.call-start = ((), (), s32[]{:S(2)}) async-start(), calls=%async_computation.30 | async-start | bytes 2654208 | tf_op jit(solution)/shard_map/reduce_scatter | solution.py:350
  1614.1 662.3 %reduce-scatter.34.cloned.1.call-start = ((), (), s32[]{:S(2)}) async-start(), calls=%async_computation.28 | async-start | bytes 2654208 | tf_op jit(solution)/shard_map/reduce_scatter | solution.py:344
  1626.4 722.8 %reduce-scatter.32.cloned.1.call-start = ((), (), s32[]{:S(2)}) async-start(), calls=%async_computation.27 | async-start | bytes 2654208 | tf_op jit(solution)/shard_map/reduce_scatter | solution.py:343
  1641.1 778.1 %reduce-scatter.30.cloned.1.call-start = ((), (), s32[]{:S(2)}) async-start(), calls=%async_computation.26 | async-start | bytes 1990656 | tf_op jit(solution)/shard_map/reduce_scatter | solution.py:340
  (217 other events, 5965.5 us)
Sparse Core Ops, SparseCore 0:
  10.2 51.9 all-gather.28
  64.4 50.2 all-gather.30
  118.8 77.1 reduce-scatter.27
  197.4 81.8 all-gather.46
  281.3 51.8 all-gather.26
  353.3 82.0 all-gather.48
  437.6 51.7 all-gather.32
  491.7 50.3 all-gather.34
  544.1 56.6 all-gather.36
  602.9 37.2 all-gather.44
  641.6 82.0 all-gather.50
  762.7 37.4 all-gather.52
  802.3 51.7 all-gather.38
  856.1 50.3 all-gather.40
  959.1 37.5 all-reduce.42
  1047.5 68.5 all-reduce.44
  1145.0 87.7 all-reduce.50
  1333.4 88.5 all-reduce.48
  1425.3 63.3 reduce-scatter.45
  1492.2 66.6 reduce-scatter.43
  1562.1 61.2 reduce-scatter.51
  1626.5 62.3 reduce-scatter.41
  1692.2 62.2 reduce-scatter.49
  1757.7 70.8 all-reduce.46
  1831.9 66.5 reduce-scatter.47
  1902.0 66.6 reduce-scatter.39
  1997.8 59.9 all-gather.42
  2062.0 68.3 reduce-scatter.35
  2134.4 68.9 reduce-scatter.37
  2207.3 68.9 reduce-scatter.33
  2280.4 68.7 reduce-scatter.31
  2353.2 65.9 reduce-scatter.29
  (3 shorter events, 76.1 us)
